TPU v7x, 32 devices: a whole 2x2x4 slice. The times are simulated.
32 devices in a mesh: seq: 16 (over z, x, core), head: 2 (over y).
Axes of the slice: x: 2, y: 2, z: 4, core: 2. Of those that a mesh axis runs over, the one named last changes fastest.
Arguments:
- points: bfloat16 [16384, 512], P(('seq', 'head')), may hold values from -5000 to 5000
- norm_gain: float32 [512], replicated, may hold values from 0.1 to 1.9
- qkv_weight: bfloat16 [3, 512, 512], replicated, may hold values from -24 to 24
- out_weight: bfloat16 [512, 512], replicated, may hold values from -4 to 4
- neighbours: int32 [64, 8], replicated, may hold values from 0 to 63, as said below
Outputs:
- update: bfloat16 [16384, 512], P(('seq', 'head'))
Inputs may be any that keep to these rules, and one draw needn't show every extreme that they name: `neighbours`: column 0 of row p is p. Columns 1 to 4 are distinct patches p + s with 0 < |s| <= 4. The last 3 columns name patches whose owner (patch // 4) is not the owner of p. Over all patches of one owner, the far columns name any one other owner at most 1 times, each time a different patch, and every owner reaches 1 with some other owner.
All inputs are finite; a program needn't handle non-finite values.
Results may differ from a plain program's by a relative error of at most 0.006.
The roundings to bfloat16 on the way count: a program that leaves them out, or rounds other values in their place, can miss the bound.
Values may be sent and summed in bfloat16 or wider, within the bound.
No kernel may reach another device: no remote copies, remote signals or barrier semaphores. Data moves between devices by JAX's collectives and lax.ppermute only.
A program may use at most 64 MiB of HBM per device.

v0:
```python
import jax
import jax.numpy as jnp
from jax import lax
from jax.sharding import PartitionSpec as P

D = 512
HEAD_DIM = 32
PATCH = 256
NEIGH = 8
NEAR = 4
FAR = 3


EPS = 1e-06


def with_halo(cells, sides, width):
    for axis, dim in sides:
        count = lax.axis_size(axis)
        ends = count - 1
        head = lax.slice_in_dim(cells, 0, width, axis=dim)
        tail = lax.slice_in_dim(cells, cells.shape[dim] - width, cells.shape[dim], axis=dim)
        cells = jnp.concatenate(
            [
                lax.ppermute(tail, axis, [(i, (i + 1) % count) for i in range(ends)]),
                cells,
                lax.ppermute(head, axis, [((i + 1) % count, i) for i in range(ends)]),
            ],
            axis=dim,
        )
    return cells


def attend_patch(operands):
    query_rows, kv_rows = operands
    local_width = query_rows.shape[1]
    local_heads = local_width // HEAD_DIM
    query_rows = query_rows.reshape(PATCH, local_heads, HEAD_DIM)
    key_rows = kv_rows[:, :local_width].reshape(-1, local_heads, HEAD_DIM)
    values = kv_rows[:, local_width:].reshape(-1, local_heads, HEAD_DIM)
    scores = jnp.einsum(
        "qhd,khd->hqk", query_rows, key_rows, preferred_element_type=jnp.float32
    ) * HEAD_DIM ** (-0.5)
    row_top = jnp.max(scores, axis=2, keepdims=True)
    lifted = jnp.exp(scores - row_top)
    weights = (lifted / jnp.sum(lifted, axis=2, keepdims=True)).astype(jnp.bfloat16)
    mixed_rows = jnp.einsum("hqk,khd->qhd", weights, values, preferred_element_type=jnp.float32)
    return mixed_rows.astype(jnp.bfloat16).reshape(PATCH, local_width)


def body(points, norm_gain, qkv_weight, out_weight, neighbours):
    head_count = lax.axis_size("head")
    head_index = lax.axis_index("head")
    seq_count = lax.axis_size("seq")
    shard_index = lax.axis_index("seq")
    column_share = D // head_count
    floats = points.astype(jnp.float32)
    mean_square = jnp.sum(floats * floats, axis=1, keepdims=True) / D
    normed = (floats * lax.rsqrt(mean_square + EPS) * norm_gain).astype(jnp.bfloat16)
    grouped_weight = (
        qkv_weight.reshape(3, D, head_count, column_share)
        .transpose(1, 2, 0, 3)
        .reshape(D, head_count, 3 * column_share)
    )
    own_columns = lax.dynamic_index_in_dim(grouped_weight, head_index, 1, keepdims=False)
    projected = jnp.dot(
        lax.all_gather(normed, "head", axis=0, tiled=True),
        own_columns,
        preferred_element_type=jnp.float32,
    ).astype(jnp.bfloat16)
    row_count = projected.shape[0]
    per_shard = row_count // PATCH
    queries = projected[:, :column_share]
    kv_local = projected[:, column_share:].reshape(per_shard, PATCH, 2 * column_share)
    extended = with_halo(kv_local, (("seq", 0),), per_shard)
    own_lists = lax.dynamic_slice_in_dim(neighbours, shard_index * per_shard, per_shard, 0)
    near_index = own_lists[:, : 1 + NEAR] - (shard_index - 1) * per_shard
    near_rows = extended[near_index]
    ref_count = per_shard * FAR
    far_lists = neighbours[:, 1 + NEAR :].reshape(seq_count, ref_count)
    owners = far_lists // per_shard
    local_ids = far_lists % per_shard
    earlier = jnp.arange(ref_count)[None, :] < jnp.arange(ref_count)[:, None]
    same_owner = owners[:, :, None] == owners[:, None, :]
    slot_ranks = jnp.sum(same_owner & earlier[None], axis=2)
    slot_count = (FAR * per_shard + seq_count - 2) // (seq_count - 1)
    owned_refs = (owners == shard_index).astype(jnp.float32)
    slot_hot = (slot_ranks[:, :, None] == jnp.arange(slot_count)[None, None, :]).astype(jnp.float32)
    local_hot = (local_ids[:, :, None] == jnp.arange(per_shard)[None, None, :]).astype(jnp.float32)
    selector = jnp.einsum("rk,rkj,rkl->rjl", owned_refs, slot_hot, local_hot).astype(jnp.bfloat16)
    flat_kv = kv_local.reshape(per_shard, PATCH * 2 * column_share)
    outgoing = jnp.dot(
        selector.reshape(seq_count * slot_count, per_shard),
        flat_kv,
        preferred_element_type=jnp.float32,
    )
    outgoing = outgoing.astype(jnp.bfloat16).reshape(seq_count, slot_count, PATCH, 2 * column_share)
    incoming = lax.all_to_all(outgoing, "seq", split_axis=0, concat_axis=0, tiled=True)
    my_owners = lax.dynamic_index_in_dim(owners, shard_index, 0, keepdims=False)
    my_slots = lax.dynamic_index_in_dim(slot_ranks, shard_index, 0, keepdims=False)
    far_rows = incoming.reshape(seq_count * slot_count, PATCH, 2 * column_share)[
        my_owners * slot_count + my_slots
    ]
    far_rows = far_rows.reshape(per_shard, FAR, PATCH, 2 * column_share)
    gathered = jnp.concatenate([near_rows, far_rows], axis=1).reshape(
        per_shard, NEIGH * PATCH, 2 * column_share
    )
    attended = lax.map(
        attend_patch, (queries.reshape(per_shard, PATCH, column_share), gathered)
    ).reshape(row_count, column_share)
    owned_rows = lax.all_to_all(attended, "head", split_axis=0, concat_axis=1, tiled=True)
    update = jnp.dot(owned_rows, out_weight, preferred_element_type=jnp.float32).astype(
        jnp.bfloat16
    )
    return update


def solution(mesh):
    placed = (P(("seq", "head"), None), P(), P(), P(), P())
    return jax.shard_map(
        body, mesh=mesh, in_specs=placed, out_specs=P(("seq", "head"), None), check_vma=False
    )
```

profile of v0, /device:TPU:16, one launch (start us, length us, event | category | flops | bytes accessed | tf_op | source)
XLA Modules:
  0.0 306.8 jit_solution(17444510389994302412)
XLA Ops:
  6.5 1.3 fusion.10
  7.8 2.0 fusion.12
  9.9 1.7 copy.56
  11.6 1.3 copy.57
  14.0 18.4 %all-gather.2.cloned.1.call-done = bf16[1024,512]{1,0:T(8,128)(2,1)} async-done(((bf16[512,512]{1,0:T(8,128)(2,1)}), bf16[1024,512]{1,0:T(8,128)(2,1)}) %all-gather.2.cloned.1.call-update) | async-done | bytes 1048592 | tf_op jit(solution)/shard_map/all_gather | solution.py:67
  32.4 2.5 convolution_convert_fusion.1
  38.2 3.5 %copy.78 = bf16[2,8,256,512]{3,2,1,0:T(8,128)(2,1)} copy(bf16[2,8,256,512]{3,1,2,0:T(8,128)(2,1)S(1)} %bitcast.71) | data formatting | bytes 8388608
  41.7 6.0 %all-to-all-start = ((bf16[16,1,256,512]{3,2,1,0:T(8,128)(2,1)}), bf16[16,1,256,512]{3,2,1,0:T(8,128)(2,1)}, u32[]{:S(2)}, u32[]{:S(2)}) async-start(bf16[16,1,256,512]{3,2,1,0:T(8,128)(2,1)} %bitcast.72), calls=%async_computation | async-start | bytes 8388608 | tf_op jit(solution)/shard_map/all_to_all | solution.py:98
  47.8 2.0 collective-permute-start
  49.8 4.6 %collective-permute-start.1 = (bf16[4,256,512]{2,1,0:T(8,128)(2,1)S(1)}, bf16[4,256,512]{2,1,0:T(8,128)(2,1)}, u32[]{:S(2)}, u32[]{:S(2)}) collective-permute-start(bf16[4,256,512]{2,1,0:T(8,128)(2,1)S(1)} %bitcast.75), channel_id=1, source_target_pairs={{2,0},{4,2},{6,4},{8,6},{10,8},{12,10},{14,12},{16,14},{18,16},{20... | collective-permute-start | bytes 3145736 | tf_op jit(solution)/shard_map/ppermute | solution.py:27
  54.9 96.6 %collective-permute-done = bf16[4,256,512]{2,1,0:T(8,128)(2,1)S(1)} collective-permute-done((bf16[4,256,512]{2,1,0:T(8,128)(2,1)S(1)}, bf16[4,256,512]{2,1,0:T(8,128)(2,1)S(1)}, u32[]{:S(2)}, u32[]{:S(2)}) %collective-permute-start) | collective-permute-done | bytes 1048608 | tf_op jit(solution)/shard_map/ppermute | solution.py:25
  151.6 2.8 pad_maximum_fusion.1
  154.4 6.0 %gather_fusion = bf16[20,256,512]{2,1,0:T(8,128)(2,1)} fusion(bf16[12,256,512]{2,1,0:T(8,128)(2,1)} %pad_maximum_fusion.1, s32[1024]{0:T(1024)S(1)} %pad_clamp_fusion.1), kind=kCustom, calls=%fused_computation | custom fusion | bytes 10485840 | tf_op jit(solution)/shard_map/gather | solution.py:78
  160.4 13.8 %copy.68 = bf16[4,5,256,512]{2,1,3,0:T(8,128)(2,1)} copy(bf16[4,5,256,512]{3,2,1,0:T(8,128)(2,1)} %bitcast.70) | data formatting | bytes 10485760 | tf_op jit(solution)/shard_map/gather | solution.py:78
  174.3 4.8 %gather_fusion.1 = bf16[12,256,512]{2,1,0:T(8,128)(2,1)} fusion(bf16[16,256,512]{2,1,0:T(8,128)(2,1)} %bitcast.16, s32[1024]{0:T(1024)S(1)} %pad_clamp_fusion), kind=kCustom, calls=%fused_computation.1 | custom fusion | bytes 6291504 | tf_op jit(solution)/shard_map/gather | solution.py:101
  179.1 7.1 %copy.69 = bf16[4,3,256,512]{2,1,3,0:T(4,128)(2,1)} copy(bf16[4,3,256,512]{3,2,1,0:T(8,128)(2,1)} %bitcast.73) | data formatting | bytes 6291456 | tf_op jit(solution)/shard_map/reshape | solution.py:104
  186.2 9.7 %pad_maximum_fusion = bf16[4,8,256,512]{2,1,3,0:T(8,128)(2,1)} fusion(bf16[4,3,256,512]{2,1,3,0:T(4,128)(2,1)} %copy.69, bf16[4,5,256,512]{2,1,3,0:T(8,128)(2,1)} %copy.68), kind=kLoop, calls=%fused_computation.16 | loop fusion | flops 16777216 | bytes 16777216 | tf_op jit(solution)/shard_map/concatenate | solution.py:105
  195.9 13.5 %reshape.188 = bf16[4,2048,512]{1,2,0:T(8,128)(2,1)} reshape(bf16[4,8,256,512]{2,1,3,0:T(8,128)(2,1)} %pad_maximum_fusion) | data formatting | bytes 16777216 | tf_op jit(solution)/shard_map/reshape | solution.py:105
  209.5 79.0 %while.10 = (s32[]{:T(128)}, bf16[4,256,256]{2,1,0:T(8,128)(2,1)}, bf16[4,2048,512]{1,2,0:T(8,128)(2,1)}, bf16[4,256,256]{2,1,0:T(8,128)(2,1)S(1)}, s32[]{:T(128)}) while((s32[]{:T(128)}, bf16[4,256,256]{2,1,0:T(8,128)(2,1)}, bf16[4,2048,512]{1,2,0:T(8,128)(2,1)}, bf16[4,256,256]{2,1,0:T(8,128)(2,1)S(1)}, s32[]{:T(128)}) %tuple.36), condition=%wide.region_5.6_spmd, body=%wide.region_2.5_spmd.sunk | while | flops 557910016 | bytes 45367876 | solution.py:108
  209.5 1.7 dynamic-slice_bitcast_fusion.2
  211.5 8.5 %fusion.44 = (f32[8,256]{1,0:T(8,128)S(1)}, f32[8,256,2048]{2,1,0:T(8,128)}) fusion(bf16[256,8,32]{0,2,1:T(8,128)(2,1)S(1)} %bitcast.78, bf16[2048,8,32]{0,2,1:T(8,128)(2,1)S(1)} %bitcast.69), kind=kOutput, calls=%fused_computation.52.clone.1 | convolution fusion | flops 281020416 | bytes 17965056 | tf_op jit(solution)/shard_map/while/body/eval_jaxpr/sub | solution.py:45
  219.9 8.5 %fusion.45 = bf16[8,32,256]{2,1,0:T(8,128)(2,1)S(1)} fusion(bf16[2048,8,32]{0,2,1:T(8,128)(2,1)S(1)} %bitcast.68, f32[8,256,2048]{2,1,0:T(8,128)} %get-tuple-element.97, f32[8,256]{1,0:T(8,128)S(1)} %get-tuple-element.98), kind=kOutput, calls=%fused_computation.11.clone.1 | convolution fusion | flops 276889600 | bytes 17965056 | tf_op jit(solution)/shard_map/while/body/eval_jaxpr/hqk,khd->qhd/dot_general | solution.py:47
  229.2 1.7 dynamic-slice_bitcast_fusion.2
  231.2 8.5 %fusion.44 = (f32[8,256]{1,0:T(8,128)S(1)}, f32[8,256,2048]{2,1,0:T(8,128)}) fusion(bf16[256,8,32]{0,2,1:T(8,128)(2,1)S(1)} %bitcast.78, bf16[2048,8,32]{0,2,1:T(8,128)(2,1)S(1)} %bitcast.69), kind=kOutput, calls=%fused_computation.52.clone.1 | convolution fusion | flops 281020416 | bytes 17965056 | tf_op jit(solution)/shard_map/while/body/eval_jaxpr/sub | solution.py:45
  239.7 8.5 %fusion.45 = bf16[8,32,256]{2,1,0:T(8,128)(2,1)S(1)} fusion(bf16[2048,8,32]{0,2,1:T(8,128)(2,1)S(1)} %bitcast.68, f32[8,256,2048]{2,1,0:T(8,128)} %get-tuple-element.97, f32[8,256]{1,0:T(8,128)S(1)} %get-tuple-element.98), kind=kOutput, calls=%fused_computation.11.clone.1 | convolution fusion | flops 276889600 | bytes 17965056 | tf_op jit(solution)/shard_map/while/body/eval_jaxpr/hqk,khd->qhd/dot_general | solution.py:47
  249.0 1.7 dynamic-slice_bitcast_fusion.2
  251.0 8.5 %fusion.44 = (f32[8,256]{1,0:T(8,128)S(1)}, f32[8,256,2048]{2,1,0:T(8,128)}) fusion(bf16[256,8,32]{0,2,1:T(8,128)(2,1)S(1)} %bitcast.78, bf16[2048,8,32]{0,2,1:T(8,128)(2,1)S(1)} %bitcast.69), kind=kOutput, calls=%fused_computation.52.clone.1 | convolution fusion | flops 281020416 | bytes 17965056 | tf_op jit(solution)/shard_map/while/body/eval_jaxpr/sub | solution.py:45
  259.4 8.5 %fusion.45 = bf16[8,32,256]{2,1,0:T(8,128)(2,1)S(1)} fusion(bf16[2048,8,32]{0,2,1:T(8,128)(2,1)S(1)} %bitcast.68, f32[8,256,2048]{2,1,0:T(8,128)} %get-tuple-element.97, f32[8,256]{1,0:T(8,128)S(1)} %get-tuple-element.98), kind=kOutput, calls=%fused_computation.11.clone.1 | convolution fusion | flops 276889600 | bytes 17965056 | tf_op jit(solution)/shard_map/while/body/eval_jaxpr/hqk,khd->qhd/dot_general | solution.py:47
  268.7 1.7 dynamic-slice_bitcast_fusion.2
  270.7 8.5 %fusion.44 = (f32[8,256]{1,0:T(8,128)S(1)}, f32[8,256,2048]{2,1,0:T(8,128)}) fusion(bf16[256,8,32]{0,2,1:T(8,128)(2,1)S(1)} %bitcast.78, bf16[2048,8,32]{0,2,1:T(8,128)(2,1)S(1)} %bitcast.69), kind=kOutput, calls=%fused_computation.52.clone.1 | convolution fusion | flops 281020416 | bytes 17965056 | tf_op jit(solution)/shard_map/while/body/eval_jaxpr/sub | solution.py:45
  279.2 8.5 %fusion.45 = bf16[8,32,256]{2,1,0:T(8,128)(2,1)S(1)} fusion(bf16[2048,8,32]{0,2,1:T(8,128)(2,1)S(1)} %bitcast.68, f32[8,256,2048]{2,1,0:T(8,128)} %get-tuple-element.97, f32[8,256]{1,0:T(8,128)S(1)} %get-tuple-element.98), kind=kOutput, calls=%fused_computation.11.clone.1 | convolution fusion | flops 276889600 | bytes 17965056 | tf_op jit(solution)/shard_map/while/body/eval_jaxpr/hqk,khd->qhd/dot_general | solution.py:47
  288.4 10.1 %all_to_all.24 = bf16[2,512,256]{2,1,0:T(8,128)(2,1)S(1)} all-to-all(bf16[2,512,256]{2,1,0:T(8,128)(2,1)} %bitcast.83), channel_id=1, replica_groups=mesh['seq'=16,'head'=2] {'head'}, dimensions={0} | all-to-all | bytes 1048576 | tf_op jit(solution)/shard_map/all_to_all | solution.py:111
  (59 shorter events, 10.6 us)
Async XLA Ops:
  6.5 292.2 %copy-start = (bf16[512,512]{1,0:T(8,128)(2,1)S(1)}, bf16[512,512]{1,0:T(8,128)(2,1)}, u32[]{:S(2)}) copy-start(bf16[512,512]{1,0:T(8,128)(2,1)} %param.10) | copy-start | bytes 1572868
  6.5 6.4 %copy-start.2 = (s32[64,8]{0,1:T(8,128)S(1)}, s32[64,8]{0,1:T(8,128)}, u32[]{:S(2)}) copy-start(s32[64,8]{0,1:T(8,128)} %param.11) | copy-start | bytes 6148
  6.5 25.9 %all-gather.2.cloned.1.call-start = ((), (), s32[]{:S(2)}) async-start(), calls=%async_computation.2 | async-start | bytes 1572864 | tf_op jit(solution)/shard_map/all_gather | solution.py:67
  34.9 1.2 copy-start.1
  41.7 132.6 %all-to-all-start = ((bf16[16,1,256,512]{3,2,1,0:T(8,128)(2,1)}), bf16[16,1,256,512]{3,2,1,0:T(8,128)(2,1)}, u32[]{:S(2)}, u32[]{:S(2)}) async-start(bf16[16,1,256,512]{3,2,1,0:T(8,128)(2,1)} %bitcast.72), calls=%async_computation | async-start | bytes 8388608 | tf_op jit(solution)/shard_map/all_to_all | solution.py:98
  47.8 103.8 %collective-permute-start = (bf16[4,256,512]{2,1,0:T(8,128)(2,1)S(1)}, bf16[4,256,512]{2,1,0:T(8,128)(2,1)S(1)}, u32[]{:S(2)}, u32[]{:S(2)}) collective-permute-start(bf16[4,256,512]{2,1,0:T(8,128)(2,1)S(1)} %bitcast.74), channel_id=1, source_target_pairs={{0,2},{2,4},{4,6},{6,8},{8,10},{10,12},{12,14},{14,16},{16,18},{18... | collective-permute-start | bytes 3145736 | tf_op jit(solution)/shard_map/ppermute | solution.py:25
  49.8 101.8 %collective-permute-start.1 = (bf16[4,256,512]{2,1,0:T(8,128)(2,1)S(1)}, bf16[4,256,512]{2,1,0:T(8,128)(2,1)}, u32[]{:S(2)}, u32[]{:S(2)}) collective-permute-start(bf16[4,256,512]{2,1,0:T(8,128)(2,1)S(1)} %bitcast.75), channel_id=1, source_target_pairs={{2,0},{4,2},{6,4},{8,6},{10,8},{12,10},{14,12},{16,14},{18,16},{20... | collective-permute-start | bytes 3145736 | tf_op jit(solution)/shard_map/ppermute | solution.py:27
  195.9 13.5 %slice-start = ((bf16[1024,768]{1,0:T(8,128)(2,1)}), bf16[1024,256]{1,0:T(8,128)(2,1)S(1)}, s32[]{:S(2)}) async-start(bf16[1024,768]{1,0:T(8,128)(2,1)} %copy-done.1), calls=%async_computation.3 | async-start | bytes 1048576 | tf_op jit(solution)/shard_map/slice | solution.py:73
Sparse Core Ops, SparseCore 0:
  10.0 22.3 all-gather.1
where the time goes:
time: 308 us; the launch traced here: 307 us
  waiting for transfers between devices  115 us (37%)
  matrix products  72.9 us (24%)
  local copies, waits for them, and re-layouts  66 us (21%)
  other arithmetic  16.5 us (5%)
  between operations  13.5 us (4%)
  starting transfers between devices  12.7 us (4%)
  blocking collectives  10.1 us (3%)
    ppermute x1, waiting for transfers between devices, with_halo(): lax.ppermute(tail, axis, [(i, (i + 1) % count) for i in range(ends)])  96.6 us
    sub x4, matrix products, attend_patch(): lifted = jnp.exp(scores - row_top)  33.9 us
    dot_general x4, matrix products, attend_patch(): jnp.einsum('hqk,khd->qhd', weights, values, preferred_element_type=jnp.fl...  33.8 us
    gather x2, local copies, waits for them, and re-layouts, body(): near_rows = extended[near_index]  19.9 us
    all_gather x1, waiting for transfers between devices, body(): lax.all_gather(normed, 'head', axis=0, tiled=True)  18.4 us
    reshape x1, local copies, waits for them, and re-layouts, body(): jnp.concatenate([near_rows, far_rows], axis=1)  13.5 us
    all_to_all x1, blocking collectives, body(): lax.all_to_all(attended, 'head', split_axis=0, concat_axis=1, tiled=True)  10.1 us
    concatenate x1, other arithmetic, body(): jnp.concatenate([near_rows, far_rows], axis=1)  9.73 us
  transfers between devices with their start and end apart: 4, of which 2 were waited for; matrix products, arithmetic and copies ran while one was open for 9% of the time, Pallas kernels for 0%

commit v1 on v0

--- a/solution.py
+++ b/solution.py
@@ -1,6 +1,11 @@
+import functools
+import math
+
 import jax
 import jax.numpy as jnp
 from jax import lax
+from jax.experimental import pallas as pl
+from jax.experimental.pallas import tpu as pltpu
 from jax.sharding import PartitionSpec as P
 
 D = 512
@@ -48,7 +53,7 @@
     return mixed_rows.astype(jnp.bfloat16).reshape(PATCH, local_width)
 
 
-def body(points, norm_gain, qkv_weight, out_weight, neighbours):
+def gathered_body(points, norm_gain, qkv_weight, out_weight, neighbours):
     head_count = lax.axis_size("head")
     head_index = lax.axis_index("head")
     seq_count = lax.axis_size("seq")
@@ -115,7 +120,240 @@
     return update
 
 
+LANES = 128
+SCALE = HEAD_DIM ** (-0.5) * math.log2(math.e)
+ROW_BY_ROW = (((1,), (1,)), ((), ()))
+VMEM = pl.BlockSpec(memory_space=pltpu.VMEM)
+SMEM = pl.BlockSpec(memory_space=pltpu.SMEM)
+
+
+def kernel_params():
+    return pltpu.CompilerParams(vmem_limit_bytes=60 * 2**20)
+
+
+def dot_bf16(rows, weight):
+    return jnp.dot(rows, weight, preferred_element_type=jnp.float32).astype(jnp.bfloat16)
+
+
+def attend_lanes(query, keys, values, tops_before=None):
+    head_of_lane = lax.broadcasted_iota(jnp.int32, (1, LANES), 1) // HEAD_DIM
+    sums = None
+    tops = jnp.zeros((query.shape[0], LANES), jnp.float32)
+    for head in range(LANES // HEAD_DIM):
+        mine = head_of_lane == head
+        masked = jnp.where(mine, query, jnp.zeros_like(query))
+        scores = [
+            lax.dot_general(masked, k, ROW_BY_ROW, preferred_element_type=jnp.float32)
+            for k in keys
+        ]
+        top = functools.reduce(jnp.maximum, scores)
+        top = jnp.max(top, axis=1, keepdims=True)
+        if tops_before is not None:
+            top = jnp.maximum(top, tops_before[:, head * HEAD_DIM : head * HEAD_DIM + 1])
+        for block, v in zip(scores, values):
+            lifted = jnp.exp2((block - top) * SCALE).astype(jnp.bfloat16)
+            mine_rows = jnp.broadcast_to(mine, v.shape)
+            wide = jnp.concatenate(
+                [jnp.where(mine, v, jnp.zeros_like(v)), mine_rows.astype(v.dtype)], axis=1
+            )
+            part = jnp.dot(lifted, wide, preferred_element_type=jnp.float32)
+            sums = part if sums is None else sums + part
+        tops = jnp.where(mine, top, tops)
+    return sums[:, :LANES], sums[:, LANES:], tops
+
+
+def block_of(index, size):
+    return pl.ds(pl.multiple_of(index * size, size), size)
+
+
+def near_kernel(pieces, own, slots, *refs):
+    count = 1 + max(piece[0] for piece in pieces)
+    arrays, (weight, mixed, total, tops, queries, keys, values) = refs[:count], refs[count:]
+    queries[...] = dot_bf16(arrays[own][...], weight[0])
+    for array, source, size, target in pieces:
+        rows = arrays[array][source : source + size, :]
+        keys[target : target + size, :] = dot_bf16(rows, weight[1])
+        values[target : target + size, :] = dot_bf16(rows, weight[2])
+    groups = queries.shape[1] // LANES
+    listed = slots.shape[1]
+
+    def step(i, carry):
+        patch, lanes = i // groups, block_of(i % groups, LANES)
+        rows = block_of(patch, PATCH)
+        spans = [block_of(slots[patch, n], PATCH) for n in range(listed)]
+        mixed[rows, lanes], total[rows, lanes], tops[rows, lanes] = attend_lanes(
+            queries[rows, lanes],
+            [keys[span, lanes] for span in spans],
+            [values[span, lanes] for span in spans],
+        )
+        return carry
+
+    lax.fori_loop(0, queries.shape[0] // PATCH * groups, step, 0)
+
+
+def near_part(slots, arrays, pieces, own, weight):
+    rows, width = arrays[own].shape
+    window = max(target + size for _, _, size, target in pieces)
+    wide = jax.ShapeDtypeStruct((rows, width), jnp.float32)
+    flops = 2 * (rows + 2 * window) * width * width + 4 * rows * slots.shape[1] * PATCH * width * 4
+    return pl.pallas_call(
+        functools.partial(near_kernel, pieces, own),
+        in_specs=[SMEM] + [VMEM] * (len(arrays) + 1),
+        out_specs=[VMEM] * 4,
+        out_shape=[wide, wide, wide, jax.ShapeDtypeStruct((rows, width), jnp.bfloat16)],
+        scratch_shapes=[pltpu.VMEM((window, width), jnp.bfloat16)] * 2,
+        compiler_params=kernel_params(),
+        cost_estimate=pl.CostEstimate(flops=flops, bytes_accessed=8 * 2**20, transcendentals=0),
+        name="near_part",
+    )(slots, *arrays, weight)
+
+
+def far_kernel(slots, halves, others, weight, out_weight, queries, mixed, total, tops, update, rows_in, keys, values, attended):
+    patches, listed = slots.shape
+    half = halves.shape[1]
+    for n in range(patches * listed):
+        rows_in[n * PATCH : n * PATCH + half, :] = halves[slots[n // listed, n % listed]]
+        rows_in[n * PATCH + half : (n + 1) * PATCH, :] = others[n]
+    for n in range(patches * listed):
+        span = slice(n * PATCH, (n + 1) * PATCH)
+        keys[span, :] = dot_bf16(rows_in[span, :], weight[1])
+        values[span, :] = dot_bf16(rows_in[span, :], weight[2])
+    groups = queries.shape[1] // LANES
+
+    def step(i, carry):
+        patch, lanes = i // groups, block_of(i % groups, LANES)
+        rows = block_of(patch, PATCH)
+        spans = [block_of(patch * listed + n, PATCH) for n in range(listed)]
+        before = tops[rows, lanes]
+        mixed_now, total_now, tops_now = attend_lanes(
+            queries[rows, lanes],
+            [keys[span, lanes] for span in spans],
+            [values[span, lanes] for span in spans],
+            before,
+        )
+        keep = jnp.exp2((before - tops_now) * SCALE)
+        mixed_now += mixed[rows, lanes] * keep
+        total_now += total[rows, lanes] * keep
+        attended[rows, lanes] = (mixed_now / total_now).astype(jnp.bfloat16)
+        return carry
+
+    lax.fori_loop(0, patches * groups, step, 0)
+    update[...] = dot_bf16(attended[...], out_weight[...])
+
+
+def far_part(slots, halves, others, weight, out_weight, state):
+    rows, width = state[0].shape
+    window = slots.shape[0] * slots.shape[1] * PATCH
+    mixed, total, tops, queries = state
+    flops = 2 * (rows + 2 * window) * width * width + 4 * rows * slots.shape[1] * PATCH * width * 4
+    return pl.pallas_call(
+        far_kernel,
+        in_specs=[SMEM] + [VMEM] * 8,
+        out_specs=VMEM,
+        out_shape=jax.ShapeDtypeStruct((rows, width), jnp.bfloat16),
+        scratch_shapes=[pltpu.VMEM((window, width), jnp.bfloat16)] * 3
+        + [pltpu.VMEM((rows, width), jnp.bfloat16)],
+        compiler_params=kernel_params(),
+        cost_estimate=pl.CostEstimate(flops=flops, bytes_accessed=8 * 2**20, transcendentals=0),
+        name="far_part",
+    )(slots, halves, others, weight, out_weight, queries, mixed, total, tops)
+
+
+def spread_kernel(picks, place, own, got, out):
+    target = pl.program_id(0)
+    patch, from_own = picks[0, target], picks[1, target]
+    half = out.shape[1]
+
+    @pl.when(from_own == 1)
+    def _():
+        start = pl.multiple_of(patch * PATCH + place[0] * half, half)
+        out[0] = own[pl.ds(start, half), :]
+
+    @pl.when(from_own == 0)
+    def _():
+        out[0] = got[patch]
+
+
+def spread(picks, place, own, got):
+    count = picks.shape[1]
+    half, width = got.shape[1:]
+    return pl.pallas_call(
+        spread_kernel,
+        grid=(count,),
+        in_specs=[SMEM, SMEM, VMEM, VMEM],
+        out_specs=pl.BlockSpec((1, half, width), lambda i: (i, 0, 0)),
+        out_shape=jax.ShapeDtypeStruct((count, half, width), jnp.bfloat16),
+        compiler_params=kernel_params(),
+        name="spread",
+    )(picks, place, own, got)
+
+
+def shifted(rows, axis, by):
+    count = lax.axis_size(axis)
+    pairs = [(i, i + by) for i in range(count) if 0 <= i + by < count]
+    return lax.ppermute(rows, axis, pairs)
+
+
+def swapped(rows):
+    return lax.ppermute(rows, "head", [(0, 1), (1, 0)])
+
+
+def paired_body(points, norm_gain, qkv_weight, out_weight, neighbours):
+    head_index = lax.axis_index("head")
+    seq_count = lax.axis_size("seq")
+    shard_index = lax.axis_index("seq")
+    rows, width = points.shape
+    patches = rows // PATCH
+    per_shard = 2 * patches
+    half = PATCH // 2
+    floats = points.astype(jnp.float32)
+    mean_square = jnp.sum(floats * floats, axis=1, keepdims=True) / D
+    normed = (floats * lax.rsqrt(mean_square + EPS) * norm_gain).astype(jnp.bfloat16)
+
+    halves = normed.reshape(patches, 2, half, width)
+    got_mine = swapped(lax.dynamic_index_in_dim(halves, 1 - head_index, 1, keepdims=False))
+    earlier = shifted(normed, "seq", 1)
+    later = shifted(normed, "seq", -1)
+    got_rest = swapped(lax.dynamic_index_in_dim(halves, head_index, 1, keepdims=False))
+    relayed = swapped(jnp.where(head_index == 0, later, earlier))
+
+    far_lists = neighbours[:, 1 + NEAR :].reshape(seq_count, per_shard * FAR)
+    owners, locals_ = far_lists // per_shard, far_lists % per_shard
+    wanted = jnp.sum(jnp.where(owners == shard_index, locals_, 0), axis=1)
+    picks = jnp.stack([wanted % patches, (wanted // patches == head_index).astype(jnp.int32)])
+    outgoing = spread(picks, head_index.reshape(1), normed, got_mine)
+    incoming = lax.all_to_all(outgoing, "seq", split_axis=0, concat_axis=0, tiled=True)
+
+    my_owners = lax.dynamic_index_in_dim(owners, shard_index, 0, keepdims=False).reshape(2, -1)
+    own_slots = lax.dynamic_index_in_dim(my_owners, head_index, 0, keepdims=False)
+    their_slots = lax.dynamic_index_in_dim(my_owners, 1 - head_index, 0, keepdims=False)
+    others = swapped(incoming[their_slots])
+
+    device = shard_index * 2 + head_index
+    near_lists = lax.dynamic_slice_in_dim(neighbours, device * patches, patches, 0)[:, : 1 + NEAR]
+    places = near_lists - (device - 2) * patches
+    block, inside = places // patches, places % patches
+    block = jnp.where((head_index == 0) & (block % 2 == 1), 4 - block, block)
+    arrays = [
+        earlier,
+        got_mine.reshape(rows // 2, width),
+        got_rest.reshape(rows // 2, width),
+        normed,
+        relayed,
+        later,
+    ]
+    pieces = [(0, 0, rows, 0), (3, 0, rows, 2 * rows), (4, 0, rows, 3 * rows), (5, 0, rows, 4 * rows)]
+    for n in range(patches):
+        pieces.append((1, n * half, half, rows + n * PATCH))
+        pieces.append((2, n * half, half, rows + n * PATCH + half))
+    state = near_part(block * patches + inside, arrays, pieces, 3, qkv_weight)
+    return far_part(
+        own_slots.reshape(patches, FAR), incoming, others, qkv_weight, out_weight, state
+    )
+
+
 def solution(mesh):
+    body = paired_body if mesh.shape["head"] == 2 else gathered_body
     placed = (P(("seq", "head"), None), P(), P(), P(), P())
     return jax.shard_map(
         body, mesh=mesh, in_specs=placed, out_specs=P(("seq", "head"), None), check_vma=False

time: 308 us -> 135 us (0.44)
  matrix products: 72.9 us -> 0 us
  local copies, waits for them, and re-layouts: 66 us -> 3.3 us
  waiting for transfers between devices: 115 us -> 56.5 us
  Pallas kernels: 0 us -> 50.8 us
  between operations: 13.5 us -> 0.09 us
  other arithmetic: 16.5 us -> 5.17 us
  blocking collectives: 10.1 us -> 0 us
  starting transfers between devices: 12.7 us -> 18 us
    pallas_call x0 -> x3, Pallas kernels: none -> 50.8 us  [the longest x1 24.2 us: near_part(): pl.pallas_call(functools.partial(near_kernel, pieces, own), in_specs=[SME...]
    ppermute x2 -> x6, waiting for transfers between devices: 96.6 us -> 56.5 us  [the longest x2 44.9 us: shifted(): return lax.ppermute(rows, axis, pairs)]
    dot_general x8 -> x0, matrix products: 39 us -> none  [the longest x4 33.8 us: attend_patch(): jnp.einsum('hqk,khd->qhd', weights, values, preferred_element_type=jnp.fl...]
    sub x4 -> x0, matrix products: 33.9 us -> none  [attend_patch(): lifted = jnp.exp(scores - row_top)]
    gather x3 -> x1, local copies, waits for them, and re-layouts: 24.7 us -> 0.6 us  [paired_body(): others = swapped(incoming[their_slots])]
    reshape x4 -> x3, local copies, waits for them, and re-layouts: 20.8 us -> 0.77 us  [the longest x1 0.62 us: paired_body(): own_slots.reshape(patches, FAR)]
    all_gather x1 -> x0, waiting for transfers between devices: 18.4 us -> none  [body(): lax.all_gather(normed, 'head', axis=0, tiled=True)]
    concatenate x2 -> x0, other arithmetic: 12.6 us -> none  [the longest x1 9.73 us: body(): jnp.concatenate([near_rows, far_rows], axis=1)]
  transfers between devices with their start and end apart: 4 -> 7, of which waited for: 2 -> 3; matrix products, arithmetic and copies ran while one was open for 9% -> 3% of each run, Pallas kernels for 0% -> 18%
where the time goes in v1:
time: 135 us; the launch traced here: 134 us
  waiting for transfers between devices  56.5 us (42%)
  Pallas kernels  50.8 us (38%)
  starting transfers between devices  18 us (13%)
  other arithmetic  5.17 us (4%)
  local copies, waits for them, and re-layouts  3.3 us (2%)
    ppermute x2, waiting for transfers between devices, shifted(): return lax.ppermute(rows, axis, pairs)  44.9 us
    pallas_call x1, Pallas kernels, near_part(): pl.pallas_call(functools.partial(near_kernel, pieces, own), in_specs=[SME...  24.2 us
    pallas_call x1, Pallas kernels, far_part(): pl.pallas_call(far_kernel, in_specs=[SMEM] + [VMEM] * 8, out_specs=VMEM,...  19.9 us
    ppermute x4, waiting for transfers between devices, swapped(): return lax.ppermute(rows, 'head', [(0, 1), (1, 0)])  11.5 us
    pallas_call x1, Pallas kernels, spread(): pl.pallas_call(spread_kernel, grid=(count,), in_specs=[SMEM, SMEM, VMEM,...  6.64 us
    ppermute x2, starting transfers between devices, shifted(): return lax.ppermute(rows, axis, pairs)  6.46 us
    all_to_all x1, starting transfers between devices, paired_body(): lax.all_to_all(outgoing, 'seq', split_axis=0, concat_axis=0, tiled=True)  6.3 us
    ppermute x4, starting transfers between devices, swapped(): return lax.ppermute(rows, 'head', [(0, 1), (1, 0)])  5.23 us
  transfers between devices with their start and end apart: 7, of which 3 were waited for; matrix products, arithmetic and copies ran while one was open for 3% of the time, Pallas kernels for 18%

profile of v1, /device:TPU:16, one launch (start us, length us, event | category | flops | bytes accessed | tf_op | source)
XLA Modules:
  0.0 133.8 jit_solution(11031526436117350226)
XLA Ops:
  0.0 1.2 fusion
  1.2 1.2 fusion.2.own.refs_3_
  2.5 0.0 copy-start
  2.5 0.8 dynamic-slice_bitcast_fusion
  3.3 1.5 %collective-permute-start = (bf16[2,128,512]{2,1,0:T(8,128)(2,1)S(1)}, bf16[2,128,512]{2,1,0:T(8,128)(2,1)S(1)}, u32[]{:S(2)}, u32[]{:S(2)}) collective-permute-start(bf16[2,128,512]{2,1,0:T(8,128)(2,1)S(1)} %get-tuple-element.14), channel_id=1, source_target_pairs={{0,1},{1,0},{2,3},{3,2},{4,5},{5,4},{6,7},{7,6},{8,9},{9,8},{10,11... | collective-permute-start | bytes 786440 | tf_op jit(solution)/shard_map/ppermute | solution.py:298
  4.9 0.1 reduce_sum.28
  4.9 0.1 reduce_sum.29
  5.1 0.6 pad_add_fusion.picks
  5.7 5.7 %collective-permute-done.got = bf16[2,128,512]{2,1,0:T(8,128)(2,1)S(1)} collective-permute-done((bf16[2,128,512]{2,1,0:T(8,128)(2,1)S(1)}, bf16[2,128,512]{2,1,0:T(8,128)(2,1)S(1)}, u32[]{:S(2)}, u32[]{:S(2)}) %collective-permute-start) | collective-permute-done | bytes 262176 | tf_op jit(solution)/shard_map/ppermute | solution.py:298
  11.4 0.7 copy-done.4
  12.1 6.6 %spread.1 = bf16[16,128,512]{2,1,0:T(8,128)(2,1)} custom-call(s32[2,16]{1,0:T(2,128)} %pad_add_fusion.picks, s32[1]{0:T(128)} %bitcast.1.place, bf16[512,512]{1,0:T(8,128)(2,1)} %copy-done, bf16[2,128,512]{2,1,0:T(8,128)(2,1)} %copy-done.4), custom_call_target="tpu_custom_call" | custom-call | tf_op jit(solution)/shard_map/spread/pallas_call | solution.py:280
  18.7 6.3 %all-to-all-start = ((bf16[16,128,512]{2,1,0:T(8,128)(2,1)}), bf16[16,128,512]{2,1,0:T(8,128)(2,1)S(1)}, u32[]{:S(2)}, u32[]{:S(2)}) async-start(bf16[16,128,512]{2,1,0:T(8,128)(2,1)} %spread.1), calls=%async_computation | async-start | bytes 4194304 | tf_op jit(solution)/shard_map/all_to_all | solution.py:325
  25.0 2.0 %collective-permute-start.2 = (bf16[512,512]{1,0:T(8,128)(2,1)S(1)}, bf16[512,512]{1,0:T(8,128)(2,1)S(1)}, u32[]{:S(2)}, u32[]{:S(2)}) collective-permute-start(bf16[512,512]{1,0:T(8,128)(2,1)S(1)} %copy-done.1), channel_id=1, source_target_pairs={{0,2},{2,4},{4,6},{6,8},{8,10},{10,12},{12,14},{14,16},{16,18},{18... | collective-permute-start | bytes 1572872 | tf_op jit(solution)/shard_map/ppermute | solution.py:294
  27.1 4.4 %collective-permute-start.4 = (bf16[512,512]{1,0:T(8,128)(2,1)S(1)}, bf16[512,512]{1,0:T(8,128)(2,1)}, u32[]{:S(2)}, u32[]{:S(2)}) collective-permute-start(bf16[512,512]{1,0:T(8,128)(2,1)S(1)} %copy-done.1), channel_id=1, source_target_pairs={{2,0},{4,2},{6,4},{8,6},{10,8},{12,10},{14,12},{16,14},{18,16},{20... | collective-permute-start | bytes 1572872 | tf_op jit(solution)/shard_map/ppermute | solution.py:294
  31.5 1.6 %collective-permute-start.3 = (bf16[2,128,512]{2,1,0:T(8,128)(2,1)}, bf16[2,128,512]{2,1,0:T(8,128)(2,1)}, u32[]{:S(2)}, u32[]{:S(2)}) collective-permute-start(bf16[2,128,512]{2,1,0:T(8,128)(2,1)} %get-tuple-element.13), channel_id=1, source_target_pairs={{0,1},{1,0},{2,3},{3,2},{4,5},{5,4},{6,7},{7,6},{8,9},{9,8},{10,11... | collective-permute-start | bytes 786440 | tf_op jit(solution)/shard_map/ppermute | solution.py:298
  33.1 0.1 copy.7
  33.2 0.1 reshape.139
  33.3 0.1 reshape.140
  33.4 44.9 %collective-permute-done.2.refs_0_ = bf16[512,512]{1,0:T(8,128)(2,1)S(1)} collective-permute-done((bf16[512,512]{1,0:T(8,128)(2,1)S(1)}, bf16[512,512]{1,0:T(8,128)(2,1)S(1)}, u32[]{:S(2)}, u32[]{:S(2)}) %collective-permute-start.2) | collective-permute-done | bytes 524320 | tf_op jit(solution)/shard_map/ppermute | solution.py:294
  78.3 1.3 broadcast_select_fusion
  79.6 0.3 collective-permute-start.5
  79.9 0.1 constant_dynamic-slice_fusion.3
  80.0 0.1 copy.10
  80.1 0.6 gather_fusion
  80.7 1.8 %collective-permute-start.1 = (bf16[6,128,512]{2,1,0:T(8,128)(2,1)S(1)}, bf16[6,128,512]{2,1,0:T(8,128)(2,1)}, u32[]{:S(2)}, u32[]{:S(2)}) collective-permute-start(bf16[6,128,512]{2,1,0:T(8,128)(2,1)S(1)} %gather_fusion), channel_id=1, source_target_pairs={{0,1},{1,0},{2,3},{3,2},{4,5},{5,4},{6,7},{7,6},{8,9},{9,8},{10,11... | collective-permute-start | bytes 2359304 | tf_op jit(solution)/shard_map/ppermute | solution.py:298
  82.6 0.6 fusion.7.slots
  83.2 0.6 reshape.141.slots
  83.8 0.0 collective-permute-done.3
  83.8 5.8 %collective-permute-done.5.refs_4_ = bf16[512,512]{1,0:T(8,128)(2,1)} collective-permute-done((bf16[512,512]{1,0:T(8,128)(2,1)S(1)}, bf16[512,512]{1,0:T(8,128)(2,1)}, u32[]{:S(2)}, u32[]{:S(2)}) %collective-permute-start.5) | collective-permute-done | bytes 524320 | tf_op jit(solution)/shard_map/ppermute | solution.py:298
  89.6 24.2 %near_part.1 = (f32[512,512]{1,0:T(8,128)}, f32[512,512]{1,0:T(8,128)}, f32[512,512]{1,0:T(8,128)}, bf16[512,512]{1,0:T(8,128)(2,1)}) custom-call(s32[2,5]{1,0:T(2,128)} %fusion.7.slots, bf16[512,512]{1,0:T(8,128)(2,1)} %copy-done.3, bf16[256,512]{1,0:T(8,128)(2,1)} %bitcast.35, bf16[256,512]{1,0:T(8,128)(2,1)} %bitcast.8.refs_2_, bf16[512,512]{1,0:T(8,128)(2,1)} %copy-done, ...), custom_call_target="tpu_custom_call" | custom-call | flops 8321499136 | bytes 8388608 | tf_op jit(solution)/shard_map/near_part/pallas_call | solution.py:199
  113.8 0.0 collective-permute-done.1.others
  113.8 19.9 %far_part.1 = bf16[512,512]{1,0:T(8,128)(2,1)} custom-call(s32[2,3]{1,0:T(2,128)} %reshape.141.slots, bf16[16,128,512]{2,1,0:T(8,128)(2,1)} %copy-done.2, bf16[6,128,512]{2,1,0:T(8,128)(2,1)} %collective-permute-done.1.others, bf16[3,512,512]{2,1,0:T(8,128)(2,1)} %weight.1, bf16[512,512]{1,0:T(8,128)(2,1)} %out_weight.1, ...), custom_call_target="tpu_custom_call" | custom-call | flops 5100273664 | bytes 8388608 | tf_op jit(solution)/shard_map/far_part/pallas_call | solution.py:249
  (22 shorter events, 0.2 us)
Async XLA Ops:
  0.0 4.8 %copy-start.5 = (s32[64,8]{0,1:T(8,128)S(1)}, s32[64,8]{0,1:T(8,128)}, u32[]{:S(2)}) copy-start(s32[64,8]{0,1:T(8,128)} %param.9) | copy-start | bytes 6148
  2.5 8.9 %copy-start = (bf16[512,512]{1,0:T(8,128)(2,1)}, bf16[512,512]{1,0:T(8,128)(2,1)S(1)}, u32[]{:S(2)}) copy-start(bf16[512,512]{1,0:T(8,128)(2,1)S(1)} %fusion.2.own.refs_3_) | copy-start | bytes 1572868
  3.3 8.0 %collective-permute-start = (bf16[2,128,512]{2,1,0:T(8,128)(2,1)S(1)}, bf16[2,128,512]{2,1,0:T(8,128)(2,1)S(1)}, u32[]{:S(2)}, u32[]{:S(2)}) collective-permute-start(bf16[2,128,512]{2,1,0:T(8,128)(2,1)S(1)} %get-tuple-element.14), channel_id=1, source_target_pairs={{0,1},{1,0},{2,3},{3,2},{4,5},{5,4},{6,7},{7,6},{8,9},{9,8},{10,11... | collective-permute-start | bytes 786440 | tf_op jit(solution)/shard_map/ppermute | solution.py:298
  11.4 0.7 copy-start.4
  18.7 6.3 %copy-start.1 = (bf16[512,512]{1,0:T(8,128)(2,1)S(1)}, bf16[512,512]{1,0:T(8,128)(2,1)}, u32[]{:S(2)}) copy-start(bf16[512,512]{1,0:T(8,128)(2,1)} %copy-done) | copy-start | bytes 1572868
  18.7 61.4 %all-to-all-start = ((bf16[16,128,512]{2,1,0:T(8,128)(2,1)}), bf16[16,128,512]{2,1,0:T(8,128)(2,1)S(1)}, u32[]{:S(2)}, u32[]{:S(2)}) async-start(bf16[16,128,512]{2,1,0:T(8,128)(2,1)} %spread.1), calls=%async_computation | async-start | bytes 4194304 | tf_op jit(solution)/shard_map/all_to_all | solution.py:325
  25.0 53.3 %collective-permute-start.2 = (bf16[512,512]{1,0:T(8,128)(2,1)S(1)}, bf16[512,512]{1,0:T(8,128)(2,1)S(1)}, u32[]{:S(2)}, u32[]{:S(2)}) collective-permute-start(bf16[512,512]{1,0:T(8,128)(2,1)S(1)} %copy-done.1), channel_id=1, source_target_pairs={{0,2},{2,4},{4,6},{6,8},{8,10},{10,12},{12,14},{14,16},{16,18},{18... | collective-permute-start | bytes 1572872 | tf_op jit(solution)/shard_map/ppermute | solution.py:294
  27.1 51.2 %collective-permute-start.4 = (bf16[512,512]{1,0:T(8,128)(2,1)S(1)}, bf16[512,512]{1,0:T(8,128)(2,1)}, u32[]{:S(2)}, u32[]{:S(2)}) collective-permute-start(bf16[512,512]{1,0:T(8,128)(2,1)S(1)} %copy-done.1), channel_id=1, source_target_pairs={{2,0},{4,2},{6,4},{8,6},{10,8},{12,10},{14,12},{16,14},{18,16},{20... | collective-permute-start | bytes 1572872 | tf_op jit(solution)/shard_map/ppermute | solution.py:294
  31.5 52.3 %collective-permute-start.3 = (bf16[2,128,512]{2,1,0:T(8,128)(2,1)}, bf16[2,128,512]{2,1,0:T(8,128)(2,1)}, u32[]{:S(2)}, u32[]{:S(2)}) collective-permute-start(bf16[2,128,512]{2,1,0:T(8,128)(2,1)} %get-tuple-element.13), channel_id=1, source_target_pairs={{0,1},{1,0},{2,3},{3,2},{4,5},{5,4},{6,7},{7,6},{8,9},{9,8},{10,11... | collective-permute-start | bytes 786440 | tf_op jit(solution)/shard_map/ppermute | solution.py:298
  78.3 1.8 %copy-start.3 = (bf16[512,512]{1,0:T(8,128)(2,1)}, bf16[512,512]{1,0:T(8,128)(2,1)S(1)}, u32[]{:S(2)}) copy-start(bf16[512,512]{1,0:T(8,128)(2,1)S(1)} %collective-permute-done.2.refs_0_) | copy-start | bytes 1572868
  79.6 10.0 %collective-permute-start.5 = (bf16[512,512]{1,0:T(8,128)(2,1)S(1)}, bf16[512,512]{1,0:T(8,128)(2,1)}, u32[]{:S(2)}, u32[]{:S(2)}) collective-permute-start(bf16[512,512]{1,0:T(8,128)(2,1)S(1)} %broadcast_select_fusion), channel_id=1, source_target_pairs={{0,1},{1,0},{2,3},{3,2},{4,5},{5,4},{6,7},{7,6},{8,9},{9,8},{10,11... | collective-permute-start | bytes 1572872 | tf_op jit(solution)/shard_map/ppermute | solution.py:298
  80.1 33.7 %copy-start.2 = (bf16[16,128,512]{2,1,0:T(8,128)(2,1)}, bf16[16,128,512]{2,1,0:T(8,128)(2,1)S(1)}, u32[]{:S(2)}) copy-start(bf16[16,128,512]{2,1,0:T(8,128)(2,1)S(1)} %all-to-all-done.halves) | copy-start | bytes 6291460
  80.7 33.1 %collective-permute-start.1 = (bf16[6,128,512]{2,1,0:T(8,128)(2,1)S(1)}, bf16[6,128,512]{2,1,0:T(8,128)(2,1)}, u32[]{:S(2)}, u32[]{:S(2)}) collective-permute-start(bf16[6,128,512]{2,1,0:T(8,128)(2,1)S(1)} %gather_fusion), channel_id=1, source_target_pairs={{0,1},{1,0},{2,3},{3,2},{4,5},{5,4},{6,7},{7,6},{8,9},{9,8},{10,11... | collective-permute-start | bytes 2359304 | tf_op jit(solution)/shard_map/ppermute | solution.py:298
